TPU v7x, 32 devices: a whole 2x2x4 slice. The times are simulated.
32 devices in a mesh: seq: 8 (over y, x, core), head: 4 (over z).
Axes of the slice: x: 2, y: 2, z: 4, core: 2. Of those that a mesh axis runs over, the one named last changes fastest.
Arguments:
- queries: bfloat16 [8192, 2048], P(('seq', 'head')), may hold values from -15 to 15
- key_rows: bfloat16 [8192, 2048], P(('seq', 'head')), may hold values from -15 to 15
- values: bfloat16 [8192, 2048], P(('seq', 'head')), may hold values from -6 to 6
- gate_logits: float32 [16], P('head'), may hold values from -1.5 to 1.5
- out_grad: bfloat16 [8192, 2048], P(('seq', 'head')), may hold values from -6 to 6
Outputs:
- output: bfloat16 [8192, 2048], P(('seq', 'head'))
- query_grad: bfloat16 [8192, 2048], P(('seq', 'head'))
- key_grad: bfloat16 [8192, 2048], P(('seq', 'head'))
- value_grad: bfloat16 [8192, 2048], P(('seq', 'head'))
All inputs are finite; a program needn't handle non-finite values.
Results may differ from a plain program's by a relative error of at most 0.0052.
The roundings to bfloat16 on the way count: a program that leaves them out, or rounds other values in their place, can miss the bound.
Values may be sent and summed in bfloat16 or wider, within the bound.
A program may use at most 128 MiB of HBM per device.

v0:
```python
import functools

import jax
import jax.numpy as jnp
from jax import lax
from jax.experimental import pallas as pl
from jax.experimental.pallas import tpu as pltpu
from jax.sharding import PartitionSpec as P

DH = 128
PAD = 8
MESH = pl.DeviceIdType.MESH
F32 = jnp.float32
BF16 = jnp.bfloat16


def feature(x):
    return jnp.where(x > 0, x + 1.0, jnp.exp(jnp.minimum(x, 0.0)))


def slope(x):
    return jnp.where(x > 0, 1.0, jnp.exp(jnp.minimum(x, 0.0)))


def split(x):
    high = x.astype(BF16)
    return high, (x - high.astype(F32)).astype(BF16)


def nn(a, b):
    return lax.dot_general(a, b, (((1,), (0,)), ((), ())), preferred_element_type=F32)


def nt(a, b):
    return lax.dot_general(a, b, (((1,), (1,)), ((), ())), preferred_element_type=F32)


def tn(a, b):
    return lax.dot_general(a, b, (((0,), (0,)), ((), ())), preferred_element_type=F32)


def kernel(
    segs,
    groups,
    heads,
    gate_ref,
    q_in,
    k_in,
    v_in,
    d_in,
    o_out,
    q_out,
    k_out,
    v_out,
    gath,
    stage,
    loc,
    fwd_mine,
    fwd_slots,
    bwd_mine,
    bwd_slots,
    carry,
    in_send,
    in_recv,
    out_send,
    out_recv,
    fwd_send,
    fwd_recv,
    bwd_send,
    bwd_recv,
):
    seg = lax.axis_index("seq")
    grp = lax.axis_index("head")
    rows = q_in.shape[0]
    length = rows * groups
    inputs = (k_in, v_in, q_in, d_in)
    outputs = (o_out, q_out, k_out, v_out)
    scale = DH ** (-0.5)
    offsets = sorted(range(1, groups), key=lambda o: abs(2 * o - groups))

    barrier = pltpu.get_barrier_semaphore()
    for o in range(1, groups):
        pl.semaphore_signal(
            barrier, inc=1, device_id=(seg, lax.rem(grp + o, groups)), device_id_type=MESH
        )

    def greet(o, c):
        pl.semaphore_signal(
            barrier, inc=1, device_id=(lax.rem(seg + o, segs), grp), device_id_type=MESH
        )
        return c

    lax.fori_loop(1, segs, greet, 0)
    pl.semaphore_wait(barrier, groups - 1 + segs - 1)

    def in_copy(a, h, dest):
        col = pl.multiple_of((dest * heads + h) * DH, DH)
        at = pl.multiple_of(grp * rows, rows)
        return (
            inputs[a].at[:, pl.ds(col, DH)],
            gath.at[a, h, pl.ds(at, rows), :],
        )

    def send_inputs(h, c):
        for a in range(4):
            for o in offsets:
                dest = lax.rem(grp + o, groups)
                src, dst = in_copy(a, h, dest)
                pltpu.make_async_remote_copy(
                    src_ref=src,
                    dst_ref=dst,
                    send_sem=in_send.at[a, h, dest],
                    recv_sem=in_recv.at[a, h, grp],
                    device_id=(seg, dest),
                    device_id_type=MESH,
                ).start()
            src, dst = in_copy(a, h, grp)
            pltpu.make_async_copy(src, dst, in_recv.at[a, h, grp]).start()
        return c

    lax.fori_loop(0, heads, send_inputs, 0)

    def wait_inputs(a, h):
        def one(z, c):
            blk = gath.at[a, h, pl.ds(pl.multiple_of(z * rows, rows), rows), :]
            pltpu.make_async_copy(blk, blk, in_recv.at[a, h, z]).wait()
            return c

        lax.fori_loop(0, groups, one, 0)

    def send_out(a, h):
        col = pl.multiple_of((grp * heads + h) * DH, DH)
        for o in offsets:
            dest = lax.rem(grp + o, groups)
            pltpu.make_async_remote_copy(
                src_ref=stage.at[a, h, pl.ds(pl.multiple_of(dest * rows, rows), rows), :],
                dst_ref=outputs[a].at[:, pl.ds(col, DH)],
                send_sem=out_send.at[a, h, dest],
                recv_sem=out_recv.at[a, h, grp],
                device_id=(seg, dest),
                device_id_type=MESH,
            ).start()
        pltpu.make_async_copy(
            stage.at[a, h, pl.ds(pl.multiple_of(grp * rows, rows), rows), :],
            outputs[a].at[:, pl.ds(col, DH)],
            out_recv.at[a, h, grp],
        ).start()

    def gate(h):
        return gate_ref[h][:1, :]

    def part_update(h):
        wait_inputs(0, h)
        wait_inputs(1, h)
        phi = feature(gath[0, h].astype(F32)).astype(BF16)
        fwd_mine[h, :DH, :] = tn(phi, gath[1, h])
        fwd_mine[h, DH:, :] = jnp.broadcast_to(
            jnp.sum(phi.astype(F32), axis=0, keepdims=True), (PAD, DH)
        )

        def one(j, c):
            pltpu.make_async_remote_copy(
                src_ref=fwd_mine.at[h],
                dst_ref=fwd_slots.at[h, seg],
                send_sem=fwd_send.at[h, j],
                recv_sem=fwd_recv.at[h, seg],
                device_id=(j, grp),
                device_id_type=MESH,
            ).start()
            return c

        lax.fori_loop(seg + 1, segs, one, 0)

    def part_local(h):
        wait_inputs(2, h)
        wait_inputs(3, h)
        rest = 1.0 - gate(h)[:, :1]
        for i in range(groups - 1, -1, -1):
            first, wide = i * rows, (i + 1) * rows
            q = gath[2, h, first:wide, :]
            d = gath[3, h, first:wide, :]
            k = gath[0, h, :wide, :]
            v = gath[1, h, :wide, :]
            s = nt(q, k) * scale
            row = lax.broadcasted_iota(jnp.int32, (rows, wide), 0) + first
            col = lax.broadcasted_iota(jnp.int32, (rows, wide), 1)
            s = jnp.where(row >= col, s, -jnp.inf)
            e = jnp.exp(s - jnp.max(s, axis=-1, keepdims=True))
            w = e * (1.0 / jnp.sum(e, axis=-1, keepdims=True))
            wb = w.astype(BF16)
            dp = nt(d, v) * rest
            ds = w * (dp - jnp.sum(w * dp, axis=-1, keepdims=True))
            dsb = ds.astype(BF16)
            loc[0, h, first:wide, :] = nn(wb, v)
            loc[1, h, first:wide, :] = nn(dsb, k)
            kg = tn(dsb, q)
            vg = tn(wb, d)
            if i == groups - 1:
                loc[2, h] = kg
                loc[3, h] = vg
            else:
                loc[2, h, :wide, :] += kg
                loc[3, h, :wide, :] += vg

    def part_memory(h):
        carry[...] = jnp.zeros_like(carry)

        def one(j, c):
            slot = fwd_slots.at[h, j]
            pltpu.make_async_copy(slot, slot, fwd_recv.at[h, j]).wait()
            carry[...] += fwd_slots[h, j]
            return c

        lax.fori_loop(0, seg, one, 0)
        memory, zsum = carry[:DH, :], carry[DH : DH + 1, :]
        high, low = split(memory)
        g = gate(h)
        update = jnp.zeros((DH, DH), F32)
        norm = jnp.zeros((1, DH), F32)
        for i in range(groups):
            here = slice(i * rows, (i + 1) * rows)
            q = gath[2, h, here, :].astype(F32)
            d = gath[3, h, here, :]
            wide = d.astype(F32)
            phi = feature(q).astype(BF16)
            phi_wide = phi.astype(F32)
            raw = jnp.sum(phi_wide * zsum, axis=-1, keepdims=True)
            inv = 1.0 / jnp.maximum(raw, 1.0)
            retrieved = (nn(phi, high) + nn(phi, low)) * inv
            factor = g * inv
            numer = factor * wide
            denom = jnp.where(
                raw > 1.0,
                -g * jnp.sum(wide * retrieved, axis=-1, keepdims=True) * inv,
                0.0,
            )
            numer_high, numer_low = split(numer)
            update = update + tn(phi, numer_high) + tn(phi, numer_low)
            norm = norm + jnp.sum(denom * phi_wide, axis=0, keepdims=True)
            stage[0, h, here, :] = (g * retrieved + (1.0 - g) * loc[0, h, here, :]).astype(BF16)
            back = (nt(d, high) + nt(d, low)) * factor + denom * zsum
            stage[1, h, here, :] = (loc[1, h, here, :] * scale + back * slope(q)).astype(BF16)
        bwd_mine[h, :DH, :] = update
        bwd_mine[h, DH:, :] = jnp.broadcast_to(norm, (PAD, DH))

        def give(j, c):
            pltpu.make_async_remote_copy(
                src_ref=bwd_mine.at[h],
                dst_ref=bwd_slots.at[h, seg],
                send_sem=bwd_send.at[h, j],
                recv_sem=bwd_recv.at[h, seg],
                device_id=(j, grp),
                device_id_type=MESH,
            ).start()
            return c

        lax.fori_loop(0, seg, give, 0)
        send_out(0, h)
        send_out(1, h)

    def part_back(h):
        carry[...] = jnp.zeros_like(carry)

        def one(j, c):
            slot = bwd_slots.at[h, j]
            pltpu.make_async_copy(slot, slot, bwd_recv.at[h, j]).wait()
            carry[...] += bwd_slots[h, j]
            return c

        lax.fori_loop(seg + 1, segs, one, 0)
        back, norm = carry[:DH, :], carry[DH : DH + 1, :]
        high, low = split(back)
        g = gate(h)
        for i in range(groups):
            here = slice(i * rows, (i + 1) * rows)
            k = gath[0, h, here, :].astype(F32)
            v = gath[1, h, here, :]
            phi = feature(k).astype(BF16)
            key = (nt(v, high) + nt(v, low) + norm) * slope(k)
            stage[2, h, here, :] = (loc[2, h, here, :] * scale + key).astype(BF16)
            value = nn(phi, high) + nn(phi, low)
            stage[3, h, here, :] = ((1.0 - g) * loc[3, h, here, :] + value).astype(BF16)
        send_out(2, h)
        send_out(3, h)

    def step(s, c):
        @pl.when(s < heads)
        def _():
            part_update(s)
            part_local(s)

        @pl.when(jnp.logical_and(s >= 1, s <= heads))
        def _():
            part_memory(s - 1)

        @pl.when(s >= 2)
        def _():
            part_back(s - 2)

        return c

    lax.fori_loop(0, heads + 2, step, 0)

    def finish(h, c):
        col = pl.multiple_of(h * DH, DH)
        for a in range(4):
            for z in range(groups):
                at = pl.multiple_of((z * heads) * DH + col, DH)
                blk = outputs[a].at[:, pl.ds(at, DH)]
                pltpu.make_async_copy(blk, blk, out_recv.at[a, h, z]).wait()
            for o in offsets:
                dest = lax.rem(grp + o, groups)
                blk = gath.at[a, h, pl.ds(0, rows), :]
                pltpu.make_async_copy(blk, blk, in_send.at[a, h, dest]).wait()
                blk = stage.at[a, h, pl.ds(0, rows), :]
                pltpu.make_async_copy(blk, blk, out_send.at[a, h, dest]).wait()

        def later(j, c):
            pltpu.make_async_copy(fwd_mine.at[h], fwd_mine.at[h], fwd_send.at[h, j]).wait()
            return c

        lax.fori_loop(seg + 1, segs, later, 0)

        def earlier(j, c):
            pltpu.make_async_copy(bwd_mine.at[h], bwd_mine.at[h], bwd_send.at[h, j]).wait()
            return c

        lax.fori_loop(0, seg, earlier, 0)
        return c

    lax.fori_loop(0, heads, finish, 0)


def body(segs, groups, queries, key_rows, values, gate_logits, out_grad):
    heads = gate_logits.shape[0]
    rows = queries.shape[0]
    length = rows * groups
    share = jnp.broadcast_to(jax.nn.sigmoid(gate_logits)[:, None, None], (heads, PAD, DH))
    any_spec = pl.BlockSpec(memory_space=pl.ANY)
    dma = pltpu.SemaphoreType.DMA
    return pl.pallas_call(
        functools.partial(kernel, segs, groups, heads),
        out_shape=[jax.ShapeDtypeStruct(queries.shape, BF16)] * 4,
        in_specs=[pl.BlockSpec(memory_space=pltpu.VMEM)] + [any_spec] * 4,
        out_specs=[any_spec] * 4,
        scratch_shapes=[
            pltpu.VMEM((4, heads, length, DH), BF16),
            pltpu.VMEM((4, heads, length, DH), BF16),
            pltpu.VMEM((4, heads, length, DH), F32),
            pltpu.VMEM((heads, DH + PAD, DH), F32),
            pltpu.VMEM((heads, segs, DH + PAD, DH), F32),
            pltpu.VMEM((heads, DH + PAD, DH), F32),
            pltpu.VMEM((heads, segs, DH + PAD, DH), F32),
            pltpu.VMEM((DH + PAD, DH), F32),
            dma((4, heads, groups)),
            dma((4, heads, groups)),
            dma((4, heads, groups)),
            dma((4, heads, groups)),
            dma((heads, segs)),
            dma((heads, segs)),
            dma((heads, segs)),
            dma((heads, segs)),
        ],
        compiler_params=pltpu.CompilerParams(collective_id=0, has_side_effects=True),
        name="infini",
    )(share, queries, key_rows, values, out_grad)


def solution(mesh):
    segs, groups = mesh.shape["seq"], mesh.shape["head"]
    tokens = P(("seq", "head"), None)
    return jax.shard_map(
        functools.partial(body, segs, groups),
        mesh=mesh,
        in_specs=(tokens, tokens, tokens, P("head"), tokens),
        out_specs=(tokens,) * 4,
        check_vma=False,
    )
```

profile of v0, /device:TPU:0, one launch (start us, length us, event | category | flops | bytes accessed | tf_op | source)
XLA Modules:
  0.0 199.7 jit_solution(16410365880829270816)
XLA Ops:
  0.6 0.7 add_divide_fusion
  1.3 0.7 broadcast_in_dim.2.gate_ref
  2.0 191.2 %infini.1 = (bf16[256,2048]{1,0:T(8,128)(2,1)}, bf16[256,2048]{1,0:T(8,128)(2,1)}, bf16[256,2048]{1,0:T(8,128)(2,1)}, bf16[256,2048]{1,0:T(8,128)(2,1)}) custom-call(f32[4,8,128]{2,1,0:T(8,128)} %broadcast_in_dim.2.gate_ref, bf16[256,2048]{1,0:T(8,128)(2,1)} %q_in.1, bf16[256,2048]{1,0:T(8,128)(2,1)} %k_in.1, bf16[256,2048]{1,0:T(8,128)(2,1)} %v_in.1, ...), custom_call_target="tpu_custom_call" | custom-call | tf_op jit(solution)/shard_map/infini/pallas_call | solution.py:341
  193.2 0.0 copy-start.2
  193.2 2.4 %copy.13 = bf16[256,2048]{1,0:T(8,128)(2,1)} copy(bf16[256,2048]{1,0:T(8,128)(2,1)} %get-tuple-element.8) | data formatting | bytes 2097152
  195.6 0.0 copy-done.2
  195.6 0.0 copy-start.1
  195.6 1.0 copy.14
  196.5 0.6 copy-done.1
  197.2 0.0 copy-start
  197.2 1.0 copy.15
  198.1 0.6 copy-done
  198.8 1.0 copy.16
Async XLA Ops:
  193.2 2.4 %copy-start.2 = (bf16[256,2048]{1,0:T(8,128)(2,1)S(1)}, bf16[256,2048]{1,0:T(8,128)(2,1)}, u32[]{:S(2)}) copy-start(bf16[256,2048]{1,0:T(8,128)(2,1)} %get-tuple-element.9) | copy-start | bytes 3145732
  195.6 1.6 copy-start.1
  197.2 1.6 copy-start
where the time goes:
time: 200 us
  Pallas kernels  191 us (96%)
  local copies, waits for them, and re-layouts  7.26 us (4%)
    pallas_call x1, Pallas kernels, body(): pl.pallas_call(functools.partial(kernel, segs, groups, heads), out_shape=...  191 us
    unnamed x10, local copies, waits for them, and re-layouts  6.57 us

commit v1 on v0

--- a/solution.py
+++ b/solution.py
@@ -147,7 +147,7 @@
         ).start()
 
     def gate(h):
-        return gate_ref[h][:1, :]
+        return 1.0 / (1.0 + jnp.exp(-jnp.full((1, DH), gate_ref[h], F32)))
 
     def part_update(h):
         wait_inputs(0, h)
@@ -331,17 +331,37 @@
     lax.fori_loop(0, heads, finish, 0)
 
 
+def place(*refs):
+    held, taken, put = refs[8:]
+    half = refs[0].shape[0] // 2
+
+    def pair(i):
+        a, at = i // 2, pl.ds((i % 2) * half, half)
+        return (
+            pltpu.make_async_copy(refs[a].at[at, :], held.at[a, at, :], taken.at[i]),
+            pltpu.make_async_copy(held.at[a, at, :], refs[4 + a].at[at, :], put.at[i]),
+        )
+
+    pairs = [pair(i) for i in range(8)]
+    for take, _ in pairs:
+        take.start()
+    for take, give in pairs:
+        take.wait()
+        give.start()
+    for _, give in pairs:
+        give.wait()
+
+
 def body(segs, groups, queries, key_rows, values, gate_logits, out_grad):
     heads = gate_logits.shape[0]
     rows = queries.shape[0]
     length = rows * groups
-    share = jnp.broadcast_to(jax.nn.sigmoid(gate_logits)[:, None, None], (heads, PAD, DH))
     any_spec = pl.BlockSpec(memory_space=pl.ANY)
     dma = pltpu.SemaphoreType.DMA
-    return pl.pallas_call(
+    results = pl.pallas_call(
         functools.partial(kernel, segs, groups, heads),
         out_shape=[jax.ShapeDtypeStruct(queries.shape, BF16)] * 4,
-        in_specs=[pl.BlockSpec(memory_space=pltpu.VMEM)] + [any_spec] * 4,
+        in_specs=[pl.BlockSpec(memory_space=pltpu.SMEM)] + [any_spec] * 4,
         out_specs=[any_spec] * 4,
         scratch_shapes=[
             pltpu.VMEM((4, heads, length, DH), BF16),
@@ -363,7 +383,15 @@
         ],
         compiler_params=pltpu.CompilerParams(collective_id=0, has_side_effects=True),
         name="infini",
-    )(share, queries, key_rows, values, out_grad)
+    )(gate_logits, queries, key_rows, values, out_grad)
+    return pl.pallas_call(
+        place,
+        out_shape=[jax.ShapeDtypeStruct(queries.shape, BF16)] * 4,
+        in_specs=[any_spec] * 4,
+        out_specs=[any_spec] * 4,
+        scratch_shapes=[pltpu.VMEM((4,) + queries.shape, BF16), dma((8,)), dma((8,))],
+        name="place",
+    )(*results)
 
 
 def solution(mesh):

time: 200 us -> 196 us (0.980)
  local copies, waits for them, and re-layouts: 7.26 us -> 0 us
  Pallas kernels: 191 us -> 195 us
    unnamed x10 -> x0, local copies, waits for them, and re-layouts: 6.57 us -> none
    pallas_call x0 -> x1, Pallas kernels: none -> 3.58 us  [body(): pl.pallas_call(place, out_shape=[jax.ShapeDtypeStruct(queries.shape, BF16...]
where the time goes in v1:
time: 196 us; the launch traced here: 195 us
  Pallas kernels  195 us (99%)
    pallas_call x1, Pallas kernels, body(): pl.pallas_call(functools.partial(kernel, segs, groups, heads), out_shape=...  191 us

profile of v1, /device:TPU:0, one launch (start us, length us, event | category | flops | bytes accessed | tf_op | source)
XLA Modules:
  0.0 195.5 jit_solution(15909170565840264099)
XLA Ops:
  0.6 191.3 %infini.1 = (bf16[256,2048]{1,0:T(8,128)(2,1)}, bf16[256,2048]{1,0:T(8,128)(2,1)}, bf16[256,2048]{1,0:T(8,128)(2,1)}, bf16[256,2048]{1,0:T(8,128)(2,1)}) custom-call(f32[4]{0:T(128)} %gate_ref.1, bf16[256,2048]{1,0:T(8,128)(2,1)} %q_in.1, bf16[256,2048]{1,0:T(8,128)(2,1)} %k_in.1, bf16[256,2048]{1,0:T(8,128)(2,1)} %v_in.1, bf16[256,2048]{1,0:T(8,128)(2,1)} %d_in.1), custom_call_target="tpu_custom_call" | custom-call | tf_op jit(solution)/shard_map/infini/pallas_call | solution.py:361
  191.9 3.6 %place.1 = (bf16[256,2048]{1,0:T(8,128)(2,1)}, bf16[256,2048]{1,0:T(8,128)(2,1)}, bf16[256,2048]{1,0:T(8,128)(2,1)}, bf16[256,2048]{1,0:T(8,128)(2,1)}) custom-call(bf16[256,2048]{1,0:T(8,128)(2,1)} %get-tuple-element.8.refs_0_, bf16[256,2048]{1,0:T(8,128)(2,1)} %get-tuple-element.9.refs_1_, bf16[256,2048]{1,0:T(8,128)(2,1)} %get-tuple-element.10.refs_2_, ...), custom_call_target="tpu_custom_call" | custom-call | tf_op jit(solution)/shard_map/place/pallas_call | solution.py:387

commit v2 on v0

--- a/solution.py
+++ b/solution.py
@@ -147,7 +147,7 @@
         ).start()
 
     def gate(h):
-        return gate_ref[h][:1, :]
+        return 1.0 / (1.0 + jnp.exp(-jnp.full((1, DH), gate_ref[h], F32)))
 
     def part_update(h):
         wait_inputs(0, h)
@@ -331,17 +331,25 @@
     lax.fori_loop(0, heads, finish, 0)
 
 
+def place(*refs):
+    done = refs[8]
+    copies = [pltpu.make_async_copy(refs[i], refs[4 + i], done.at[i]) for i in range(4)]
+    for copy in copies:
+        copy.start()
+    for copy in copies:
+        copy.wait()
+
+
 def body(segs, groups, queries, key_rows, values, gate_logits, out_grad):
     heads = gate_logits.shape[0]
     rows = queries.shape[0]
     length = rows * groups
-    share = jnp.broadcast_to(jax.nn.sigmoid(gate_logits)[:, None, None], (heads, PAD, DH))
     any_spec = pl.BlockSpec(memory_space=pl.ANY)
     dma = pltpu.SemaphoreType.DMA
-    return pl.pallas_call(
+    results = pl.pallas_call(
         functools.partial(kernel, segs, groups, heads),
         out_shape=[jax.ShapeDtypeStruct(queries.shape, BF16)] * 4,
-        in_specs=[pl.BlockSpec(memory_space=pltpu.VMEM)] + [any_spec] * 4,
+        in_specs=[pl.BlockSpec(memory_space=pltpu.SMEM)] + [any_spec] * 4,
         out_specs=[any_spec] * 4,
         scratch_shapes=[
             pltpu.VMEM((4, heads, length, DH), BF16),
@@ -361,9 +369,18 @@
             dma((heads, segs)),
             dma((heads, segs)),
         ],
-        compiler_params=pltpu.CompilerParams(collective_id=0, has_side_effects=True),
+        compiler_params=pltpu.CompilerParams(collective_id=0, has_side_effects=True, vmem_limit_bytes=49 * 1024 * 1024),
         name="infini",
-    )(share, queries, key_rows, values, out_grad)
+    )(gate_logits, queries, key_rows, values, out_grad)
+    return pl.pallas_call(
+        place,
+        out_shape=[jax.ShapeDtypeStruct(queries.shape, BF16)] * 4,
+        in_specs=[any_spec] * 4,
+        out_specs=[pl.BlockSpec(memory_space=pltpu.HBM)] * 4,
+        scratch_shapes=[dma((4,))],
+        compiler_params=pltpu.CompilerParams(vmem_limit_bytes=4 * 1024 * 1024),
+        name="place",
+    )(*results)
 
 
 def solution(mesh):

time: 200 us -> 194 us (0.970)
  local copies, waits for them, and re-layouts: 7.26 us -> 0.65 us
  Pallas kernels: 191 us -> 193 us
    unnamed x10 -> x2, local copies, waits for them, and re-layouts: 6.57 us -> 0.65 us
    pallas_call x0 -> x1, Pallas kernels: none -> 2.04 us  [body(): pl.pallas_call(place, out_shape=[jax.ShapeDtypeStruct(queries.shape, BF16...]
where the time goes in v2:
time: 194 us
  Pallas kernels  193 us (99%)
    pallas_call x1, Pallas kernels, body(): pl.pallas_call(functools.partial(kernel, segs, groups, heads), out_shape=...  191 us

profile of v2, /device:TPU:0, one launch (start us, length us, event | category | flops | bytes accessed | tf_op | source)
XLA Modules:
  0.0 194.3 jit_solution(15726079709485764610)
XLA Ops:
  0.6 0.0 copy-start
  0.6 0.6 copy-done
  1.3 191.0 %infini.1 = (bf16[256,2048]{1,0:T(8,128)(2,1)S(1)}, bf16[256,2048]{1,0:T(8,128)(2,1)S(1)}, bf16[256,2048]{1,0:T(8,128)(2,1)S(1)}, bf16[256,2048]{1,0:T(8,128)(2,1)S(1)}) custom-call(f32[4]{0:T(128)S(1)} %copy-done, bf16[256,2048]{1,0:T(8,128)(2,1)} %q_in.1, bf16[256,2048]{1,0:T(8,128)(2,1)} %k_in.1, bf16[256,2048]{1,0:T(8,128)(2,1)} %v_in.1, ...), custom_call_target="tpu_custom_call" | custom-call | tf_op jit(solution)/shard_map/infini/pallas_call | solution.py:349
  192.3 2.0 %place.1 = (bf16[256,2048]{1,0:T(8,128)(2,1)}, bf16[256,2048]{1,0:T(8,128)(2,1)}, bf16[256,2048]{1,0:T(8,128)(2,1)}, bf16[256,2048]{1,0:T(8,128)(2,1)}) custom-call(bf16[256,2048]{1,0:T(8,128)(2,1)S(1)} %get-tuple-element.8.refs_0_, bf16[256,2048]{1,0:T(8,128)(2,1)S(1)} %get-tuple-element.9.refs_1_, bf16[256,2048]{1,0:T(8,128)(2,1)S(1)} %get-tuple-element.10.refs_2_, ...), custom_call_target="tpu_custom_call" | custom-call | tf_op jit(solution)/shard_map/place/pallas_call | solution.py:375
Async XLA Ops:
  0.6 0.7 copy-start
